TPU v7x, 128 devices: a whole 4x4x4 slice. The times are simulated.
128 devices in a mesh: enc: 8 (over x, core), dp: 16 (over z, y).
Axes of the slice: x: 4, y: 4, z: 4, core: 2. Of those that a mesh axis runs over, the one named last changes fastest.
Arguments:
- patches: bfloat16 [16, 128, 64, 1280], P('dp', 'enc'), may hold values from -6 to 6
- cotangent: bfloat16 [16, 128, 64, 1280], P('dp', 'enc'), may hold values from -6 to 6
- block_dest: int32 [16, 128], P('dp', 'enc'), may hold values from -1 to 7, as said below
- window_len: int32 [16, 128], P('dp', 'enc'), may hold values from 1 to 64, as said below
- ln_gain: float32 [1280], replicated, may hold values from 0.5 to 1.5
- ln_bias: float32 [1280], replicated, may hold values from -3 to 3
- qkv_weight: bfloat16 [1280, 3840], replicated, may hold values from -4 to 4
- qkv_scale: float32 [3840], replicated, may hold values from 0.01 to 0.04
- qkv_bias: float32 [3840], replicated, may hold values from -3 to 3
- out_weight: bfloat16 [1280, 1280], replicated, may hold values from -4 to 4
- out_scale: float32 [1280], replicated, may hold values from 0.01 to 0.04
- out_bias: float32 [1280], replicated, may hold values from -3 to 3
Outputs:
- embeddings: bfloat16 [16, 128, 64, 1280], P('dp', 'enc')
- patch_grad: bfloat16 [16, 128, 64, 1280], P('dp', 'enc')
- qkv_weight_grad: float32 [1280, 3840], P(('enc', 'dp'))
- out_weight_grad: float32 [1280, 1280], P(('enc', 'dp'))
Inputs may be any that keep to these rules, and one draw needn't show every extreme that they name: `block_dest`: in each data group the live blocks of each enc index come first in its 16 slots; every enc index of a group is the destination of exactly 8 blocks of that group, at most 2 from any one enc index, and some enc index sends exactly 2 to one destination; some enc index holds 16 live blocks. `window_len`: some window is full.
All inputs are finite; a program needn't handle non-finite values.
Results may differ from a plain program's by a relative error of at most 0.0098.
Values may be sent and summed in bfloat16 or wider, within the bound.
No kernel may reach another device: no remote copies, remote signals or barrier semaphores. Data moves between devices by JAX's collectives and lax.ppermute only.
A program may use at most 192 MiB of HBM per device.

v0:
```python
import jax
import jax.numpy as jnp
from jax import lax
from jax.sharding import PartitionSpec as P

HEADS = 16
RECV = 8


def contract(form, left, right):
    return jnp.einsum(form, left, right, preferred_element_type=jnp.float32)


def window_layer(
    patches,
    lengths,
    cotangent,
    ln_gain,
    ln_bias,
    qkv_weight,
    qkv_scale,
    qkv_bias,
    out_weight,
    out_scale,
    out_bias,
    heads,
):
    blocks, window, width = patches.shape
    head_dim = width // heads
    scale = 1.0 / head_dim**0.5
    position = jnp.arange(window, dtype=jnp.int32)
    row_mask = (position[None, :] < lengths[:, None]).astype(jnp.float32)
    key_mask = (position[None, :] < jnp.maximum(lengths, 1)[:, None]).astype(jnp.float32)
    inputs = patches.astype(jnp.float32)
    centered = inputs - jnp.mean(inputs, axis=-1, keepdims=True)
    inv_std = lax.rsqrt(jnp.mean(centered * centered, axis=-1, keepdims=True) + 1e-06)
    normed = centered * inv_std
    hidden = (normed * ln_gain + ln_bias).astype(jnp.bfloat16)
    flat_hidden = hidden.reshape(blocks * window, width)
    projected = jnp.dot(flat_hidden, qkv_weight, preferred_element_type=jnp.float32)
    qkv = (
        (projected * qkv_scale + qkv_bias)
        .astype(jnp.bfloat16)
        .reshape(blocks, window, 3, heads, head_dim)
    )
    query = qkv[:, :, 0]
    keys = qkv[:, :, 1]
    values = qkv[:, :, 2]
    scores = contract("bqhd,bkhd->bhqk", query, keys) * scale
    raised = jnp.exp(scores) * key_mask[:, None, None, :]
    probs = raised / jnp.sum(raised, axis=-1, keepdims=True)
    probs_low = probs.astype(jnp.bfloat16)
    attended = contract("bhqk,bkhd->bqhd", probs_low, values).astype(jnp.bfloat16)
    flat_att = attended.reshape(blocks * window, width)
    output = (
        jnp.dot(flat_att, out_weight, preferred_element_type=jnp.float32) * out_scale + out_bias
    )
    output = output.reshape(blocks, window, width) + inputs
    embeddings = (output * row_mask[:, :, None]).astype(jnp.bfloat16)
    grad_out = cotangent.astype(jnp.float32) * row_mask[:, :, None]
    grad_scaled = (grad_out * out_scale).astype(jnp.bfloat16)
    flat_grad = grad_scaled.reshape(blocks * window, width)
    out_grad = lax.dot_general(
        flat_att, flat_grad, (((0,), (0,)), ((), ())), preferred_element_type=jnp.float32
    )
    grad_att = lax.dot_general(
        flat_grad, out_weight, (((1,), (1,)), ((), ())), preferred_element_type=jnp.float32
    )
    grad_att = grad_att.astype(jnp.bfloat16).reshape(blocks, window, heads, head_dim)
    grad_probs = contract("bqhd,bkhd->bhqk", grad_att, values)
    grad_values = contract("bhqk,bqhd->bkhd", probs_low, grad_att)
    grad_scores = probs * (grad_probs - jnp.sum(probs * grad_probs, axis=-1, keepdims=True))
    grad_low = (grad_scores * scale).astype(jnp.bfloat16)
    grad_query = contract("bhqk,bkhd->bqhd", grad_low, keys)
    grad_keys = contract("bhqk,bqhd->bkhd", grad_low, query)
    grad_qkv = jnp.stack([grad_query, grad_keys, grad_values], axis=2).reshape(
        blocks * window, 3 * width
    )
    grad_qkv = (grad_qkv * qkv_scale).astype(jnp.bfloat16)
    qkv_grad = lax.dot_general(
        flat_hidden, grad_qkv, (((0,), (0,)), ((), ())), preferred_element_type=jnp.float32
    )
    grad_hidden = lax.dot_general(
        grad_qkv, qkv_weight, (((1,), (1,)), ((), ())), preferred_element_type=jnp.float32
    )
    grad_normed = grad_hidden.reshape(blocks, window, width) * ln_gain
    grad_ln = inv_std * (
        grad_normed
        - jnp.mean(grad_normed, axis=-1, keepdims=True)
        - normed * jnp.mean(grad_normed * normed, axis=-1, keepdims=True)
    )
    patch_grad = ((grad_out + grad_ln) * row_mask[:, :, None]).astype(jnp.bfloat16)
    return (embeddings, patch_grad, qkv_grad, out_grad)


def per_device(
    patches,
    cotangent,
    block_dest,
    window_len,
    ln_gain,
    ln_bias,
    qkv_weight,
    qkv_scale,
    qkv_bias,
    out_weight,
    out_scale,
    out_bias,
):
    params = (
        ln_gain,
        ln_bias,
        qkv_weight,
        qkv_scale,
        qkv_bias,
        out_weight,
        out_scale,
        out_bias,
        HEADS,
    )
    local_x = patches[0]
    local_dy = cotangent[0]
    dest = block_dest[0]
    lengths = jnp.where(dest >= 0, window_len[0], 0)
    held, window, width = local_x.shape
    groups = lax.axis_size("enc")
    most = max(2, 2 * RECV // groups)
    slots = groups * most
    slot_ids = jnp.arange(slots, dtype=jnp.int32)
    held_ids = jnp.arange(held, dtype=jnp.int32)
    earlier = (dest[:, None] == dest[None, :]) & (held_ids[None, :] < held_ids[:, None])
    rank = jnp.sum(earlier.astype(jnp.int32), axis=1)
    target = jnp.where(dest >= 0, dest * most + rank, -1)
    match = target[None, :] == slot_ids[:, None]
    source_of = jnp.sum(jnp.where(match, held_ids[None, :], 0), axis=1)
    filled = jnp.any(match, axis=1)
    send_x = jnp.where(filled[:, None, None], local_x[source_of], 0).reshape(
        groups, most, window, width
    )
    send_dy = jnp.where(filled[:, None, None], local_dy[source_of], 0).reshape(
        groups, most, window, width
    )
    send_len = jnp.where(filled, lengths[source_of], 0).astype(jnp.bfloat16).reshape(groups, most)
    got_x, got_dy, got_len = (
        lax.all_to_all(send_x, "enc", split_axis=0, concat_axis=0, tiled=True),
        lax.all_to_all(send_dy, "enc", split_axis=0, concat_axis=0, tiled=True),
        lax.all_to_all(send_len, "enc", split_axis=0, concat_axis=0, tiled=True),
    )
    got_len = got_len.reshape(slots).astype(jnp.int32)
    live = got_len > 0
    order = jnp.cumsum(live.astype(jnp.int32)) - 1
    pick = (order[None, :] == jnp.arange(RECV, dtype=jnp.int32)[:, None]) & live[None, :]
    chosen = jnp.sum(jnp.where(pick, slot_ids[None, :], 0), axis=1)
    work_x = got_x.reshape(slots, window, width)[chosen]
    work_dy = got_dy.reshape(slots, window, width)[chosen]
    emb, pgrad, qkv_grad, out_grad = window_layer(work_x, got_len[chosen], work_dy, *params)
    back_index = jnp.clip(order, 0, RECV - 1)
    ret_emb = jnp.where(live[:, None, None], emb[back_index], 0).reshape(
        groups, most, window, width
    )
    ret_grad = jnp.where(live[:, None, None], pgrad[back_index], 0).reshape(
        groups, most, window, width
    )
    home_emb, home_grad = (
        lax.all_to_all(ret_emb, "enc", split_axis=0, concat_axis=0, tiled=True),
        lax.all_to_all(ret_grad, "enc", split_axis=0, concat_axis=0, tiled=True),
    )
    home_index = jnp.clip(target, 0, slots - 1)
    embeddings = jnp.where(
        (dest >= 0)[:, None, None], home_emb.reshape(slots, window, width)[home_index], 0
    )
    patch_grad = jnp.where(
        (dest >= 0)[:, None, None], home_grad.reshape(slots, window, width)[home_index], 0
    )
    qkv_grad, out_grad = (
        lax.psum_scatter(qkv_grad, ("enc", "dp"), scatter_dimension=0, tiled=True),
        lax.psum_scatter(out_grad, ("enc", "dp"), scatter_dimension=0, tiled=True),
    )
    return (embeddings[None], patch_grad[None], qkv_grad, out_grad)


def solution(mesh):
    placed = (
        P("dp", "enc", None, None),
        P("dp", "enc", None, None),
        P("dp", "enc"),
        P("dp", "enc"),
        P(),
        P(),
        P(),
        P(),
        P(),
        P(),
        P(),
        P(),
    )
    return jax.shard_map(
        per_device,
        mesh=mesh,
        in_specs=placed,
        out_specs=(
            P("dp", "enc", None, None),
            P("dp", "enc", None, None),
            P(("enc", "dp"), None),
            P(("enc", "dp"), None),
        ),
        check_vma=False,
    )
```

profile of v0, /device:TPU:1, one launch (start us, length us, event | category | flops | bytes accessed | tf_op | source)
XLA Modules:
  0.0 553.9 jit_solution(4063249823922849565)
XLA Ops:
  7.2 1.0 convert_reduce_fusion.1
  8.2 0.7 multiply_bitcast_fusion
  8.8 0.1 select_reduce_fusion
  9.0 0.1 fusion.42
  9.2 0.1 fusion.39
  9.3 0.7 bitcast_select_fusion.2
  10.0 0.7 gather_fusion
  10.6 0.7 convert_element_type.223
  11.3 5.8 %all-to-all-start = ((bf16[8,1,2]{2,1,0:T(2,128)(2,1)}), bf16[8,1,2]{2,1,0:T(2,128)(2,1)S(1)}, u32[]{:S(2)}, u32[]{:S(2)}) async-start(bf16[8,1,2]{2,1,0:T(2,128)(2,1)} %convert_element_type.223), calls=%async_computation | async-start | bytes 8192 | tf_op jit(solution)/shard_map/all_to_all | solution.py:147
  17.2 3.9 gather_fusion.6
  21.2 3.9 gather_fusion.1
  25.1 5.3 broadcast_select_fusion
  30.4 4.9 all-to-all-start.1
  35.6 0.1 fusion.40
  35.8 0.1 select_reduce_fusion.1
  35.9 0.6 gather_fusion.3
  36.8 30.5 %all-to-all-done.1 = bf16[8,2,64,1280]{3,2,1,0:T(8,128)(2,1)} async-done(((bf16[8,2,64,1280]{3,2,1,0:T(8,128)(2,1)}), bf16[8,2,64,1280]{3,2,1,0:T(8,128)(2,1)}, u32[]{:S(2)}, u32[]{:S(2)}) %all-to-all-start.1) | async-done | bytes 2621472 | tf_op jit(solution)/shard_map/all_to_all | solution.py:145
  67.3 5.2 all-to-all-start.3
  72.5 3.5 gather_fusion.2
  76.0 1.6 convert_reduce_fusion
  77.6 1.8 multiply_reduce_fusion.2
  79.5 1.9 fusion.18
  81.4 10.7 %add_convert_fusion = bf16[512,3840]{1,0:T(8,128)(2,1)} fusion(bf16[512,1280]{1,0:T(8,128)(2,1)S(1)} %fusion.18, bf16[1280,3840]{1,0:T(8,128)(2,1)} %param.18, f32[3840]{0:T(1024)S(1)} %copy-done.13, f32[3840]{0:T(1024)S(1)} %copy-done.11), kind=kOutput, calls=%fused_computation.16 | convolution fusion | flops 5039063040 | bytes 15104000 | tf_op jit(solution)/shard_map/dot_general | solution.py:40
  92.1 12.9 %reshape.512 = bf16[8,64,3,16,80]{4,3,2,1,0:T(8,128)(2,1)} reshape(bf16[512,3840]{1,0:T(8,128)(2,1)} %add_convert_fusion) | data formatting | bytes 7864320 | tf_op jit(solution)/shard_map/reshape | solution.py:44
  105.0 6.2 %fusion.60 = (bf16[8,64,1,16,80]{4,3,2,1,0:T(8,128)(2,1)}, bf16[8,64,1,16,80]{4,3,2,1,0:T(8,128)(2,1)}, bf16[8,64,1,16,80]{4,3,2,1,0:T(8,128)(2,1)}) fusion(bf16[8,64,3,16,80]{4,3,2,1,0:T(8,128)(2,1)} %reshape.512), kind=kLoop, calls=%fused_computation.117 | loop fusion | bytes 7864320 | tf_op jit(solution)/shard_map/slice | solution.py:47
  111.2 3.5 gather_fusion.7
  114.7 1.7 fusion.14
  116.4 3.0 convolution_convert_fusion
  119.3 5.4 reshape.517
  124.8 5.6 %fusion.33 = f32[8,16,64,64]{2,3,1,0:T(8,128)} fusion(bf16[8,64,1,16,80]{4,3,2,1,0:T(8,128)(2,1)} %get-tuple-element.16, bf16[8,64,16,80]{3,2,1,0:T(8,128)(2,1)} %reshape.517), kind=kOutput, calls=%fused_computation.61 | convolution fusion | flops 83886080 | bytes 4718592 | tf_op jit(solution)/shard_map/bqhd,bkhd->bhqk/dot_general | solution.py:11
  130.4 1.7 fusion.9
  132.1 1.9 copy-done.15
  134.0 2.9 convert_bitcast_fusion
  136.9 11.2 %fusion.25 = f32[8,64,1,16,80]{4,1,3,0,2:T(8,128)} fusion(f32[8,16,64,64]{2,3,1,0:T(8,128)} %fusion.33, bf16[8,64,1,16,80]{4,3,2,1,0:T(8,128)(2,1)} %get-tuple-element.14, f32[8,16,64,64]{2,3,1,0:T(8,128)} %copy-done.15, f32[8,16,64]{2,1,0:T(8,128)S(1)} %get-tuple-element.29, f32[8,64]{1,0:T(8,128)S(1)} %fusion.45), kind=kOutput, calls=%fused_computation.52 | convolution fusion | flops 89661504 | bytes 8161280 | tf_op jit(solution)/shard_map/bhqk,bkhd->bqhd/dot_general | solution.py:11
  148.1 11.1 %fusion.28 = f32[8,64,1,16,80]{4,1,3,0,2:T(8,128)} fusion(f32[8,16,64,64]{2,3,1,0:T(8,128)} %fusion.33, bf16[8,64,1,16,80]{4,3,2,1,0:T(8,128)(2,1)} %get-tuple-element.15, f32[8,16,64,64]{2,3,1,0:T(8,128)} %copy-done.15, f32[8,16,64]{2,1,0:T(8,128)S(1)} %get-tuple-element.29, f32[8,64]{1,0:T(8,128)S(1)} %fusion.45), kind=kOutput, calls=%fused_computation.53 | convolution fusion | flops 89661504 | bytes 8161280 | tf_op jit(solution)/shard_map/bhqk,bqhd->bkhd/dot_general | solution.py:11
  159.2 6.2 %convolution_bitcast_fusion = f32[8,64,1,16,80]{4,1,3,0,2:T(8,128)} fusion(bf16[8,64,16,80]{3,2,1,0:T(8,128)(2,1)} %reshape.517, f32[8,16,64,64]{2,3,1,0:T(8,128)} %copy-done.15, f32[8,16,64]{2,1,0:T(8,128)S(1)} %get-tuple-element.29, f32[8,64]{1,0:T(8,128)S(1)} %fusion.45), kind=kOutput, calls=%fused_computation.54 | convolution fusion | flops 85983232 | bytes 6064128 | tf_op jit(solution)/shard_map/bhqk,bqhd->bkhd/dot_general | solution.py:11
  165.4 2.9 copy.82
  168.3 4.5 reshape.513
  172.9 12.2 %multiply_convert_fusion = (bf16[8,64,3,16,80]{4,1,3,0,2:T(8,128)(2,1)}, f32[8,64,3,16,80]{4,1,3,0,2:T(8,128)}) fusion(f32[3,16,80]{2,1,0:T(8,128)S(1)} %mul.223, f32[8,64,1,16,80]{4,1,3,0,2:T(8,128)} %convolution_bitcast_fusion, f32[8,64,1,16,80]{4,1,3,0,2:T(8,128)} %fusion.28, f32[8,64,1,16,80]{4,1,3,0,2:T(8,128)} %fusion.25), kind=kLoop, calls=%fused_computation.12 | loop fusion | flops 7864320 | bytes 19676160 | tf_op jit(solution)/shard_map/convert_element_type | solution.py:79
  185.1 16.1 %copy.89 = f32[8,64,3,16,80]{4,3,2,1,0:T(8,128)} copy(f32[8,64,3,16,80]{4,1,3,0,2:T(8,128)} %get-tuple-element.13) | data formatting | bytes 15728640 | tf_op jit(solution)/shard_map/stack | solution.py:76
  201.2 12.9 %reshape.518 = f32[8,64,3840]{2,1,0:T(8,128)} reshape(f32[8,64,3,16,80]{4,3,2,1,0:T(8,128)} %copy.89) | data formatting | bytes 15728640 | tf_op jit(solution)/shard_map/reshape | solution.py:76
  214.1 11.3 %fusion.59 = (f32[8,64]{1,0:T(8,128)S(1)}, f32[8,64]{1,0:T(8,128)S(1)}, f32[8,64,1280]{2,1,0:T(8,128)S(1)}) fusion(f32[8,64]{1,0:T(8,128)S(1)} %add_rsqrt_fusion, f32[8,64]{1,0:T(8,128)S(1)} %broadcast_multiply_fusion.2, bf16[8,64,1280]{2,1,0:T(8,128)(2,1)} %gather_fusion.2, f32[1280]{0:T(1024)S(1)} %copy-done.9, bf16[1280,3840]{1,0:T(8,128)(2,1)} %param.18, ...), kind=kOutput, calls=%fused_computation.116 | convolution fusion | flops 5041683456 | bytes 21655552 | tf_op jit(solution)/shard_map/dot_general | solution.py:83
  225.5 1.9 fusion.10
  227.4 3.1 add_convert_fusion.1
  230.5 4.6 fusion.62
  235.1 6.9 %copy.90 = bf16[8,64,3,16,80]{4,3,2,1,0:T(8,128)(2,1)} copy(bf16[8,64,3,16,80]{4,1,3,0,2:T(8,128)(2,1)S(1)} %bitcast.110) | data formatting | bytes 7864320 | tf_op jit(solution)/shard_map/convert_element_type | solution.py:79
  242.0 10.5 %convert_element_type.215 = bf16[512,3840]{1,0:T(8,128)(2,1)} reshape(bf16[8,64,3,16,80]{4,3,2,1,0:T(8,128)(2,1)} %copy.90) | data formatting | bytes 7864320 | tf_op jit(solution)/shard_map/convert_element_type | solution.py:79
  252.5 12.0 %fusion.61 = f32[1280,3840]{1,0:T(8,128)} fusion(bf16[512,1280]{1,0:T(8,128)(2,1)} %bitcast.119, bf16[512,3840]{1,0:T(8,128)(2,1)} %convert_element_type.215), kind=kOutput, calls=%fused_computation.118 | convolution fusion | flops 5033164800 | bytes 24903680 | tf_op jit(solution)/shard_map/dot_general | solution.py:80
  264.5 0.1 copy.75
  264.6 0.1 copy.76
  264.8 3.5 gather_fusion.4
  268.3 3.5 gather_fusion.8
  271.8 4.7 broadcast_select_fusion.2
  276.5 49.0 %all_to_all.26 = bf16[8,2,64,1280]{3,2,1,0:T(8,128)(2,1)} all-to-all(bf16[8,2,64,1280]{3,2,1,0:T(8,128)(2,1)S(1)} %get-tuple-element.22), channel_id=1, replica_groups=mesh['enc'=8,'dp'=16] {'enc'}, dimensions={0} | all-to-all | bytes 5242880 | tf_op jit(solution)/shard_map/all_to_all | solution.py:165
  325.5 5.5 all-to-all-start.4
  331.2 0.1 copy.85
  331.3 0.1 fusion.41
  331.4 4.5 gather_fusion.5
  335.9 40.4 %all-to-all-done.4 = bf16[8,2,64,1280]{3,2,1,0:T(8,128)(2,1)} async-done(((bf16[8,2,64,1280]{3,2,1,0:T(8,128)(2,1)}), bf16[8,2,64,1280]{3,2,1,0:T(8,128)(2,1)}, u32[]{:S(2)}, u32[]{:S(2)}) %all-to-all-start.4) | async-done | bytes 2621472 | tf_op jit(solution)/shard_map/all_to_all | solution.py:166
  376.4 3.9 gather_fusion.9
  380.3 5.6 %bitcast_select_fusion = (bf16[1,16,64,1280]{3,2,1,0:T(8,128)(2,1)}, bf16[1,16,64,1280]{3,2,1,0:T(8,128)(2,1)}) fusion(bf16[16,64,1280]{2,1,0:T(8,128)(2,1)} %gather_fusion.9, pred[16]{0:T(512)(128)(4,1)S(1)} %broadcast_compare_fusion.1, bf16[16,64,1280]{2,1,0:T(8,128)(2,1)} %gather_fusion.5), kind=kLoop, calls=%fused_computation.28 | loop fusion | flops 2621440 | bytes 10485776 | tf_op jit(solution)/shard_map/jit(_where)/select_n | solution.py:172
  385.9 157.5 %all-reduce.5.cloned.1.call-done = (f32[1280,3840]{1,0:T(8,128)}, f32[1280,1280]{1,0:T(8,128)}) async-done(((f32[1280,3840]{1,0:T(8,128)}, f32[1280,1280]{1,0:T(8,128)}), (f32[1280,3840]{1,0:T(8,128)}, f32[1280,1280]{1,0:T(8,128)})) %all-reduce.5.cloned.1.call-update) | async-done | bytes 26214416
  543.4 1.7 constant_dynamic-slice_fusion.1
  545.1 1.5 constant_dynamic-slice_fusion
  (68 shorter events, 1.2 us)
Async XLA Ops:
  7.2 109.2 %copy-start = (bf16[1280,1280]{1,0:T(8,128)(2,1)S(1)}, bf16[1280,1280]{1,0:T(8,128)(2,1)}, u32[]{:S(2)}) copy-start(bf16[1280,1280]{1,0:T(8,128)(2,1)} %param.21) | copy-start | bytes 9830404
  11.3 19.1 %all-to-all-start = ((bf16[8,1,2]{2,1,0:T(2,128)(2,1)}), bf16[8,1,2]{2,1,0:T(2,128)(2,1)S(1)}, u32[]{:S(2)}, u32[]{:S(2)}) async-start(bf16[8,1,2]{2,1,0:T(2,128)(2,1)} %convert_element_type.223), calls=%async_computation | async-start | bytes 8192 | tf_op jit(solution)/shard_map/all_to_all | solution.py:147
  30.4 4.9 copy-start.11
  30.4 36.9 %all-to-all-start.1 = ((bf16[8,2,64,1280]{3,2,1,0:T(8,128)(2,1)}), bf16[8,2,64,1280]{3,2,1,0:T(8,128)(2,1)}, u32[]{:S(2)}, u32[]{:S(2)}) async-start(bf16[8,2,64,1280]{3,2,1,0:T(8,128)(2,1)} %get-tuple-element.24), calls=%async_computation.1 | async-start | bytes 5242880 | tf_op jit(solution)/shard_map/all_to_all | solution.py:145
  67.3 43.9 %all-to-all-start.3 = ((bf16[8,2,64,1280]{3,2,1,0:T(8,128)(2,1)}), bf16[8,2,64,1280]{3,2,1,0:T(8,128)(2,1)}, u32[]{:S(2)}, u32[]{:S(2)}) async-start(bf16[8,2,64,1280]{3,2,1,0:T(8,128)(2,1)} %get-tuple-element.23), calls=%async_computation.3 | async-start | bytes 5242880 | tf_op jit(solution)/shard_map/all_to_all | solution.py:146
  72.5 470.9 %all-reduce.5.cloned.1.call-start = ((), (), s32[]{:S(2)}) async-start(), calls=%async_computation.5 | async-start | bytes 52428800
  72.5 7.0 %copy-start.8 = (f32[1280]{0:T(1024)S(1)}, f32[1280]{0:T(1024)}, u32[]{:S(2)}) copy-start(f32[1280]{0:T(1024)} %param.17) | copy-start | bytes 15364
  72.5 7.0 %copy-start.9 = (f32[1280]{0:T(1024)S(1)}, f32[1280]{0:T(1024)}, u32[]{:S(2)}) copy-start(f32[1280]{0:T(1024)} %param.16) | copy-start | bytes 15364
  76.0 5.4 copy-start.13
  111.2 3.5 copy-start.10
  124.8 5.6 %copy-start.5 = (bf16[8,64,1,16,80]{4,3,2,1,0:T(8,128)(2,1)S(1)}, bf16[8,64,1,16,80]{4,3,2,1,0:T(8,128)(2,1)}, u32[]{:S(2)}) copy-start(bf16[8,64,1,16,80]{4,3,2,1,0:T(8,128)(2,1)} %get-tuple-element.15) | copy-start | bytes 3932164
  124.8 5.6 %copy-start.6 = (bf16[8,64,1,16,80]{4,3,2,1,0:T(8,128)(2,1)S(1)}, bf16[8,64,1,16,80]{4,3,2,1,0:T(8,128)(2,1)}, u32[]{:S(2)}) copy-start(bf16[8,64,1,16,80]{4,3,2,1,0:T(8,128)(2,1)} %get-tuple-element.14) | copy-start | bytes 3932164
  130.4 3.6 copy-start.3
  132.1 1.9 copy-start.15
  159.2 6.2 %copy-start.4 = (bf16[8,64,16,80]{3,1,2,0:T(8,128)(2,1)S(1)}, bf16[8,64,16,80]{3,1,2,0:T(8,128)(2,1)}, u32[]{:S(2)}) copy-start(bf16[8,64,16,80]{3,1,2,0:T(8,128)(2,1)} %convert_bitcast_fusion) | copy-start | bytes 3932164
  214.1 11.3 %copy-start.7 = (bf16[512,1280]{1,0:T(8,128)(2,1)S(1)}, bf16[512,1280]{1,0:T(8,128)(2,1)}, u32[]{:S(2)}) copy-start(bf16[512,1280]{1,0:T(8,128)(2,1)} %reshape.513) | copy-start | bytes 3932164
  214.1 11.3 %copy-start.14 = (f32[1280]{0:T(1024)S(1)}, f32[1280]{0:T(1024)}, u32[]{:S(2)}) copy-start(f32[1280]{0:T(1024)} %param.23) | copy-start | bytes 15364
  225.4 1.9 copy-start.1
  225.4 1.9 copy-start.2
  225.5 9.6 %slice-start = ((s8[6291456]{0:T(1024)(128)(4,1)}), s8[4194304]{0:T(1024)(128)(4,1)S(1)}, s32[]{:S(2)}) async-start(s8[6291456]{0:T(1024)(128)(4,1)} %bitcast.109), calls=%async_computation.6 | async-start | bytes 8388608
  227.4 7.7 %slice-start.1 = ((s8[6291456]{0:T(1024)(128)(4,1)}), s8[2097152]{0:T(1024)(128)(4,1)S(1)}, s32[]{:S(2)}) async-start(s8[6291456]{0:T(1024)(128)(4,1)} %bitcast.109), calls=%async_computation.7 | async-start | bytes 4194304
  325.5 5.7 %copy-start.12 = (s32[1,16]{1,0:T(1,128)S(1)}, s32[1,16]{1,0:T(1,128)}, u32[]{:S(2)}) copy-start(s32[1,16]{1,0:T(1,128)} %param.14) | copy-start | bytes 196
  325.5 50.9 %all-to-all-start.4 = ((bf16[8,2,64,1280]{3,2,1,0:T(8,128)(2,1)}), bf16[8,2,64,1280]{3,2,1,0:T(8,128)(2,1)}, u32[]{:S(2)}, u32[]{:S(2)}) async-start(bf16[8,2,64,1280]{3,2,1,0:T(8,128)(2,1)} %get-tuple-element.21), calls=%async_computation.4 | async-start | bytes 5242880 | tf_op jit(solution)/shard_map/all_to_all | solution.py:166
Sparse Core Ops, SparseCore 0:
  264.6 278.7 all-reduce.4
where the time goes:
time: 563 us; the launch traced here: 554 us
  waiting for transfers between devices  228 us (40%)
  local copies, waits for them, and re-layouts  117 us (21%)
  matrix products  82.1 us (15%)
  blocking collectives  49 us (9%)
  other arithmetic  41.1 us (7%)
  starting transfers between devices  21.5 us (4%)
  between operations  14.7 us (3%)
    unnamed x2, waiting for transfers between devices  158 us
    all_to_all x1, blocking collectives, per_device(): lax.all_to_all(ret_emb, 'enc', split_axis=0, concat_axis=0, tiled=True)  49 us
    all_to_all x1, waiting for transfers between devices, per_device(): lax.all_to_all(ret_grad, 'enc', split_axis=0, concat_axis=0, tiled=True)  40.4 us
    dot_general x6, matrix products, contract(): return jnp.einsum(form, left, right, preferred_element_type=jnp.float32)  38.7 us
    all_to_all x1, waiting for transfers between devices, per_device(): lax.all_to_all(send_x, 'enc', split_axis=0, concat_axis=0, tiled=True)  30.5 us
    convert_element_type x2, local copies, waits for them, and re-layouts, window_layer(): grad_qkv = (grad_qkv * qkv_scale).astype(jnp.bfloat16)  17.4 us
    another operation x1, local copies, waits for them, and re-layouts, window_layer(): jnp.stack([grad_query, grad_keys, grad_values], axis=2)  16.1 us
    reshape x1, local copies, waits for them, and re-layouts, window_layer(): jnp.stack([grad_query, grad_keys, grad_values], axis=2)  12.9 us
  transfers between devices with their start and end apart: 5, of which 3 were waited for; matrix products, arithmetic and copies ran while one was open for 14% of the time, Pallas kernels for 0%

commit v1 on v0

v1 whole, which is shorter than its diff:
```python
import jax
import jax.numpy as jnp
from jax import lax
from jax.experimental import pallas as pl
from jax.experimental.pallas import tpu as pltpu
from jax.sharding import PartitionSpec as P

D = 1280
HEADS = 16
WIN = 64
TM = 256
HALF = 640
NHP = 4
SCALE = 1.0 / 80**0.5
BF = jnp.bfloat16
F32 = jnp.float32
VMEM = 60 * 1024 * 1024


def nn(a, b):
    return lax.dot_general(a, b, (((1,), (0,)), ((), ())), preferred_element_type=F32)


def nt(a, b):
    return lax.dot_general(a, b, (((1,), (1,)), ((), ())), preferred_element_type=F32)


def lanes(shape):
    return lax.broadcasted_iota(jnp.int32, shape, 1)


def head_masks(i):
    lane = lanes((1, 256))
    lo = 32 * i
    in_a = (lane >= lo) & (lane < lo + 80)
    in_b = (lane >= lo + 80) & (lane < lo + 160)
    return in_a, in_b


def stack_heads(win, in_a, in_b):
    zero = jnp.zeros_like(win)
    return jnp.concatenate([jnp.where(in_a, win, zero), jnp.where(in_b, win, zero)], axis=0)


def pack(s):
    even = (lanes((64, 256)) // 64) % 2 == 0
    return jnp.where(even, s[:64], s[64:])


def unpack(p):
    even = (lanes((64, 256)) // 64) % 2 == 0
    zero = jnp.zeros_like(p)
    return jnp.concatenate([jnp.where(even, p, zero), jnp.where(even, zero, p)], axis=0)


def segment_ones():
    r = lax.broadcasted_iota(jnp.int32, (256, 256), 0) // 64
    c = lax.broadcasted_iota(jnp.int32, (256, 256), 1) // 64
    return jnp.where(r == c, 1.0, 0.0).astype(BF)


def segment_sum(x, ones):
    hi = x.astype(BF)
    lo = (x - hi.astype(F32)).astype(BF)
    return nn(hi, ones) + nn(lo, ones)


def pair_transpose(full):
    return jnp.concatenate([full[:, :128].T, full[:, 128:].T], axis=1)


def join_windows(w):
    tiles = [w[0][:, :128]]
    for i in range(1, NHP):
        tiles.append(w[i - 1][:, 128:] + w[i][:, :128])
    tiles.append(w[NHP - 1][:, 128:])
    return jnp.concatenate(tiles, axis=1)


def row_order(core):
    r = lax.broadcasted_iota(jnp.int32, (D, D), 0)
    c = lax.broadcasted_iota(jnp.int32, (D, D), 1)
    side = r // 640
    rest = r % 640
    d = rest // 40
    x = (rest % 40) // 10
    j = rest % 10
    e = 2 * x + jnp.bitwise_xor(core, side)
    return jnp.where(c == 160 * e + 10 * d + j, 1.0, 0.0).astype(BF)


def forward_body(
    core_ref, x_ref, dy_ref, rm_ref, km_ref, gain_ref, bias_ref, w_ref, qs_ref, qb_ref,
    os_ref, qkv_ref, p_ref, att_ref, gs_ref, ht_ref, keep_ref, send_ref,
    perm_ref, ones_ref, attt_ref, gsall_ref,
):
    step = pl.program_id(0)

    @pl.when(step == 0)
    def _():
        perm_ref[...] = row_order(core_ref[0])
        ones_ref[...] = segment_ones()

    @pl.when(step < 4)
    def _():
        x = x_ref[...].astype(F32)
        cen = x - jnp.mean(x, axis=-1, keepdims=True)
        inv = lax.rsqrt(jnp.mean(cen * cen, axis=-1, keepdims=True) + 1e-06)
        hidden = (cen * inv * gain_ref[...] + bias_ref[...]).astype(BF)
        ht_ref[...] = nt(perm_ref[...], hidden).astype(BF)
        gs = (dy_ref[...].astype(F32) * rm_ref[...] * os_ref[...]).astype(BF)
        gs_ref[...] = gs
        row = pl.multiple_of(step * TM, TM)
        gsall_ref[pl.ds(row, TM), :] = gs
        for c in range(6):
            cols = slice(c * HALF, (c + 1) * HALF)
            acc = nn(hidden, w_ref[:, cols])
            qkv_ref[:, cols] = (acc * qs_ref[:, cols] + qb_ref[:, cols]).astype(BF)
        ones = ones_ref[...]
        for b in range(2):
            rows = slice(b * 128, (b + 1) * 128)
            km = km_ref[b]
            for g in range(2):
                outs = []
                for i in range(NHP):
                    in_a, in_b = head_masks(i)
                    lo = g * HALF + 128 * i
                    q = qkv_ref[rows, lo : lo + 256]
                    k = qkv_ref[rows, D + lo : D + lo + 256]
                    v = qkv_ref[rows, 2 * D + lo : 2 * D + lo + 256]
                    s = pack(nt(q, stack_heads(k, in_a, in_b)))
                    e = jnp.exp(s * SCALE) * km
                    p = e / segment_sum(e, ones)
                    p_ref[b, g * NHP + i] = p
                    outs.append(nn(unpack(p.astype(BF)), stack_heads(v, in_a, in_b)))
                att_ref[rows, g * HALF : (g + 1) * HALF] = join_windows(outs).astype(BF)
        attt_ref[:, pl.ds(row, TM)] = nt(perm_ref[...], att_ref[...]).astype(BF)

    @pl.when((step >= 4) & (step < 6))
    def _():
        row = pl.multiple_of((step - 4) * 320, 320)
        keep_ref[...] = nn(attt_ref[pl.ds(row, 320), :], gsall_ref[...]).astype(BF)

    @pl.when(step >= 6)
    def _():
        row = pl.multiple_of((step - 4) * 320, 320)
        send_ref[...] = nn(attt_ref[pl.ds(row, 320), :], gsall_ref[...]).astype(BF)


def whole(shape):
    return pl.BlockSpec(shape, lambda i: tuple(0 for _ in shape), pipeline_mode=pl.Buffered(1))


def params():
    return pltpu.CompilerParams(
        dimension_semantics=("arbitrary",), vmem_limit_bytes=VMEM
    )


def forward_call(core, x, dy, rm, km, gain, bias, w, qs, qb, osc):
    t = x.shape[0]
    tile = lambda i: jnp.minimum(i, 3)
    rows = lambda n: pl.BlockSpec((TM, n), lambda i: (tile(i), 0))
    return pl.pallas_call(
        forward_body,
        grid=(8,),
        in_specs=[
            pl.BlockSpec(memory_space=pltpu.SMEM),
            rows(D), rows(D), rows(1),
            pl.BlockSpec((2, 1, 256), lambda i: (tile(i), 0, 0)),
            whole((1, D)), whole((1, D)), whole((D, 3 * D)),
            whole((1, 3 * D)), whole((1, 3 * D)), whole((1, D)),
        ],
        out_specs=[
            rows(3 * D),
            pl.BlockSpec((2, 8, 64, 256), lambda i: (tile(i), 0, 0, 0)),
            rows(D), rows(D),
            pl.BlockSpec((D, TM), lambda i: (0, tile(i))),
            pl.BlockSpec((320, D), lambda i: (jnp.clip(i - 4, 0, 1), 0)),
            pl.BlockSpec((320, D), lambda i: (jnp.clip(i - 6, 0, 1), 0)),
        ],
        out_shape=[
            jax.ShapeDtypeStruct((t, 3 * D), BF),
            jax.ShapeDtypeStruct((t // 128, 8, 64, 256), F32),
            jax.ShapeDtypeStruct((t, D), BF),
            jax.ShapeDtypeStruct((t, D), BF),
            jax.ShapeDtypeStruct((D, t), BF),
            jax.ShapeDtypeStruct((640, D), BF),
            jax.ShapeDtypeStruct((640, D), BF),
        ],
        scratch_shapes=[
            pltpu.VMEM((D, D), BF),
            pltpu.VMEM((256, 256), BF),
            pltpu.VMEM((D, t), BF),
            pltpu.VMEM((t, D), BF),
        ],
        compiler_params=params(),
        cost_estimate=pl.CostEstimate(
            flops=20 * 10**9, transcendentals=10**6, bytes_accessed=40 * 10**6
        ),
        name="forward",
    )(core, x, dy, rm, km, gain, bias, w, qs, qb, osc)


def backward_body(
    q_ref, k_ref, v_ref, gs_ref, wo_ref, p_ref, sq_ref, sk_ref, sv_ref, ht_ref,
    gq_ref, gk_ref, gv_ref, keep_ref, send_ref, ga_ref, all_ref, ones_ref,
):
    step = pl.program_id(0)

    @pl.when(step == 0)
    def _():
        ones_ref[...] = segment_ones()

    @pl.when(step < 4)
    def _():
        ga_ref[...] = nt(gs_ref[...], wo_ref[...]).astype(BF)
        ones = ones_ref[...]
        for b in range(2):
            rows = slice(b * 128, (b + 1) * 128)
            at = pl.multiple_of(step * TM + b * 128, 128)
            gqs, gks, gvs = [], [], []
            for i in range(NHP):
                in_a, in_b = head_masks(i)
                cols = slice(128 * i, 128 * i + 256)
                q, k, v, ga = q_ref[rows, cols], k_ref[rows, cols], v_ref[rows, cols], ga_ref[rows, cols]
                p = p_ref[b, i]
                gp = pack(nt(ga, stack_heads(v, in_a, in_b)))
                t = p * gp
                g = unpack((p * (gp - segment_sum(t, ones)) * SCALE).astype(BF))
                pf = unpack(p.astype(BF))
                gqs.append(nn(g, stack_heads(k, in_a, in_b)))
                gks.append(nn(pair_transpose(g), stack_heads(q, in_a, in_b)))
                gvs.append(nn(pair_transpose(pf), stack_heads(ga, in_a, in_b)))
            for n, (ws, s_ref, o_ref) in enumerate(
                ((gqs, sq_ref, gq_ref), (gks, sk_ref, gk_ref), (gvs, sv_ref, gv_ref))
            ):
                val = (join_windows(ws) * s_ref[...]).astype(BF)
                o_ref[rows, :] = val
                all_ref[pl.ds(at, 128), n * HALF : (n + 1) * HALF] = val

    @pl.when((step >= 4) & (step < 6))
    def _():
        row = pl.multiple_of((step - 4) * 320, 320)
        keep_ref[...] = nn(ht_ref[pl.ds(row, 320), :], all_ref[...]).astype(BF)

    @pl.when(step >= 6)
    def _():
        row = pl.multiple_of((step - 4) * 320, 320)
        send_ref[...] = nn(ht_ref[pl.ds(row, 320), :], all_ref[...]).astype(BF)


def backward_call(half, qkv, gs, wo, p, qs, ht):
    t = gs.shape[0]
    tile = lambda i: jnp.minimum(i, 3)
    third = lambda n: pl.BlockSpec((TM, HALF), lambda i: (tile(i), 2 * n + half))
    sc = lambda n: pl.BlockSpec((1, HALF), lambda i: (0, 2 * n + half))
    return pl.pallas_call(
        backward_body,
        grid=(8,),
        in_specs=[
            third(0), third(1), third(2),
            pl.BlockSpec((TM, D), lambda i: (tile(i), 0)),
            pl.BlockSpec((HALF, D), lambda i: (half, 0), pipeline_mode=pl.Buffered(1)),
            pl.BlockSpec((2, NHP, 64, 256), lambda i: (tile(i), half, 0, 0)),
            sc(0), sc(1), sc(2),
            whole((D, t)),
        ],
        out_specs=[
            pl.BlockSpec((TM, HALF), lambda i: (tile(i), 0)),
            pl.BlockSpec((TM, HALF), lambda i: (tile(i), 0)),
            pl.BlockSpec((TM, HALF), lambda i: (tile(i), 0)),
            pl.BlockSpec((320, 3 * HALF), lambda i: (jnp.clip(i - 4, 0, 1), 0)),
            pl.BlockSpec((320, 3 * HALF), lambda i: (jnp.clip(i - 6, 0, 1), 0)),
        ],
        out_shape=[jax.ShapeDtypeStruct((t, HALF), BF)] * 3
        + [jax.ShapeDtypeStruct((640, 3 * HALF), BF)] * 2,
        scratch_shapes=[
            pltpu.VMEM((TM, HALF), BF),
            pltpu.VMEM((t, 3 * HALF), BF),
            pltpu.VMEM((256, 256), BF),
        ],
        compiler_params=params(),
        cost_estimate=pl.CostEstimate(
            flops=8 * 10**9, transcendentals=0, bytes_accessed=30 * 10**6
        ),
        name="backward%d" % half,
    )(qkv, qkv, qkv, gs, wo, p, qs, qs, qs, ht)


def finish_body(
    x_ref, dy_ref, rm_ref, att_ref, g0_ref, g1_ref, g2_ref, g3_ref, g4_ref, g5_ref,
    gain_ref, w_ref, wo_ref, os_ref, ob_ref, emb_ref, pg_ref,
):
    rm = rm_ref[...]
    x = x_ref[...].astype(F32)
    out = nn(att_ref[...], wo_ref[...]) * os_ref[...] + ob_ref[...] + x
    emb_ref[...] = (out * rm).astype(BF)
    cen = x - jnp.mean(x, axis=-1, keepdims=True)
    inv = lax.rsqrt(jnp.mean(cen * cen, axis=-1, keepdims=True) + 1e-06)
    normed = cen * inv
    gh = None
    for c, r in enumerate((g0_ref, g1_ref, g2_ref, g3_ref, g4_ref, g5_ref)):
        part = nt(r[...], w_ref[:, c * HALF : (c + 1) * HALF])
        gh = part if gh is None else gh + part
    gn = gh * gain_ref[...]
    gl = inv * (
        gn
        - jnp.mean(gn, axis=-1, keepdims=True)
        - normed * jnp.mean(gn * normed, axis=-1, keepdims=True)
    )
    go = dy_ref[...].astype(F32) * rm
    pg_ref[...] = ((go + gl) * rm).astype(BF)


def finish_call(x, dy, rm, att, parts, gain, w, wo, osc, ob):
    t = x.shape[0]
    rows = lambda n: pl.BlockSpec((TM, n), lambda i: (i, 0))
    return pl.pallas_call(
        finish_body,
        grid=(t // TM,),
        in_specs=[rows(D), rows(D), rows(1), rows(D)]
        + [rows(HALF)] * 6
        + [whole((1, D)), whole((D, 3 * D)), whole((D, D)), whole((1, D)), whole((1, D))],
        out_specs=[rows(D), rows(D)],
        out_shape=[jax.ShapeDtypeStruct((t, D), BF)] * 2,
        compiler_params=params(),
        cost_estimate=pl.CostEstimate(
            flops=14 * 10**9, transcendentals=0, bytes_accessed=30 * 10**6
        ),
        name="finish",
    )(x, dy, rm, att, *parts, gain, w, wo, osc, ob)


def local_masks(dest, window_len):
    lengths = jnp.where(dest >= 0, window_len, 0)
    pos = jnp.arange(WIN, dtype=jnp.int32)
    rm = (pos[None, :] < lengths[:, None]).astype(F32).reshape(-1, 1)
    km = (pos[None, :] < jnp.maximum(lengths, 1)[:, None]).astype(F32)
    km = km.reshape(-1, 1, 128)
    return rm, jnp.concatenate([km, km], axis=2)


def reduce_piece(keep, send):
    swap = [(i, i ^ 1) for i in range(8)]
    got = lax.ppermute(send, "enc", swap)
    total = (keep + got).reshape(16, 40, -1)
    return lax.psum_scatter(total, "dp", scatter_dimension=0, tiled=True)[0]


def local_work(core, x, dy, dest, wl, gain, bias, w, qs, qb, wo, osc, ob, reduce):
    rm, km = local_masks(dest, wl)
    row = lambda a: a.reshape(1, -1)
    gain, bias, qs, qb, osc, ob = map(row, (gain, bias, qs, qb, osc, ob))
    qkv, p, att, gs, ht, okeep, osend = forward_call(
        core, x, dy, rm, km, gain, bias, w, qs, qb, osc
    )
    red_o = reduce(okeep, osend)
    gq0, gk0, gv0, keep0, send0 = backward_call(0, qkv, gs, wo, p, qs, ht)
    red_0 = reduce(keep0, send0)
    gq1, gk1, gv1, keep1, send1 = backward_call(1, qkv, gs, wo, p, qs, ht)
    red_1 = reduce(keep1, send1)
    emb, pg = finish_call(
        x, dy, rm, att, (gq0, gq1, gk0, gk1, gv0, gv1), gain, w, wo, osc, ob
    )
    return emb, pg, red_o, red_0, red_1


def per_device(x, dy, dest, wl, gain, bias, w, qs, qb, wo, osc, ob):
    core = (lax.axis_index("enc") % 2).reshape(1).astype(jnp.int32)
    shape = x.shape
    emb, pg, red_o, red_0, red_1 = local_work(
        core, x.reshape(-1, D), dy.reshape(-1, D), dest[0], wl[0],
        gain, bias, w, qs, qb, wo, osc, ob, reduce_piece,
    )
    both = jnp.concatenate([red_o, red_0, red_1], axis=1).astype(F32)
    both = both.reshape(4, 10, 4 * D)
    groups = [[0, 2, 4, 6], [1, 3, 5, 7]]
    mine = lax.psum_scatter(
        both, "enc", scatter_dimension=0, axis_index_groups=groups, tiled=True
    )[0]
    halves = mine[:, D:].reshape(10, 2, 3, HALF)
    qkv_grad = halves.transpose(0, 2, 1, 3).reshape(10, 3 * D)
    return emb.reshape(shape), pg.reshape(shape), qkv_grad, mine[:, :D]


def solution(mesh):
    big = P("dp", "enc", None, None)
    small = P("dp", "enc")
    return jax.shard_map(
        per_device,
        mesh=mesh,
        in_specs=(big, big, small, small) + (P(),) * 8,
        out_specs=(big, big, P(("enc", "dp"), None), P(("enc", "dp"), None)),
        check_vma=False,
    )
```

time: 563 us -> 357 us (0.63); the launches traced: 554 us -> 356 us
  Pallas kernels: 0 us -> 142 us
  local copies, waits for them, and re-layouts: 117 us -> 15.7 us
  matrix products: 82.1 us -> 0 us
  waiting for transfers between devices: 228 us -> 169 us
  blocking collectives: 49 us -> 0 us
  other arithmetic: 41.1 us -> 12.7 us
  starting transfers between devices: 21.5 us -> 2.6 us
    pallas_call x0 -> x4, Pallas kernels: none -> 142 us  [the longest x1 58.7 us: forward_call(): pl.pallas_call(forward_body, grid=(8,), in_specs=[pl.BlockSpec(memory_spa...]
    dot_general x12 -> x0, matrix products: 82.1 us -> none  [the longest x6 38.7 us: contract(): return jnp.einsum(form, left, right, preferred_element_type=jnp.float32)]
    all_to_all x4 -> x0, waiting for transfers between devices: 70.9 us -> none  [the longest x1 40.4 us: per_device(): lax.all_to_all(ret_grad, 'enc', split_axis=0, concat_axis=0, tiled=True)]
    all_to_all x1 -> x0, blocking collectives: 49 us -> none  [per_device(): lax.all_to_all(ret_emb, 'enc', split_axis=0, concat_axis=0, tiled=True)]
    gather x10 -> x0, local copies, waits for them, and re-layouts: 31.6 us -> none  [the longest x1 4.5 us: per_device(): home_emb.reshape(slots, window, width)[home_index]]
    reshape x4 -> x8, local copies, waits for them, and re-layouts: 35.7 us -> 8.05 us  [the longest x6 7.15 us: local_work(): row = lambda a: a.reshape(1, -1)]
    all_to_all x4 -> x0, starting transfers between devices: 21.5 us -> none  [the longest x1 5.79 us: per_device(): lax.all_to_all(send_len, 'enc', split_axis=0, concat_axis=0, tiled=True)]
    convert_element_type x7 -> x1, local copies, waits for them, and re-layouts: 21.2 us -> 1.26 us  [local_masks(): rm = (pos[None, :] < lengths[:, None]).astype(F32).reshape(-1, 1)]
  transfers between devices with their start and end apart: 5 -> 7, of which waited for: 3 -> 6; matrix products, arithmetic and copies ran while one was open for 14% -> 3% of each run, Pallas kernels for 0% -> 23%
where the time goes in v1:
time: 357 us; the launch traced here: 356 us
  waiting for transfers between devices  169 us (47%)
  Pallas kernels  142 us (40%)
  local copies, waits for them, and re-layouts  15.7 us (4%)
  between operations  13.8 us (4%)
  other arithmetic  12.7 us (4%)
    unnamed x7, waiting for transfers between devices  157 us
    pallas_call x1, Pallas kernels, forward_call(): pl.pallas_call(forward_body, grid=(8,), in_specs=[pl.BlockSpec(memory_spa...  58.7 us
    pallas_call x2, Pallas kernels, backward_call(): pl.pallas_call(backward_body, grid=(8,), in_specs=[third(0), third(1), th...  57 us
    pallas_call x1, Pallas kernels, finish_call(): pl.pallas_call(finish_body, grid=(t // TM,), in_specs=[rows(D), rows(D),...  26.2 us
    ppermute x3, waiting for transfers between devices, reduce_piece(): got = lax.ppermute(send, 'enc', swap)  12.5 us
    add x3, other arithmetic, reduce_piece(): total = (keep + got).reshape(16, 40, -1)  10.7 us
    reshape x6, local copies, waits for them, and re-layouts, local_work(): row = lambda a: a.reshape(1, -1)  7.15 us
  transfers between devices with their start and end apart: 7, of which 6 were waited for; matrix products, arithmetic and copies ran while one was open for 3% of the time, Pallas kernels for 23%

profile of v1, /device:TPU:1, one launch (start us, length us, event | category | flops | bytes accessed | tf_op | source)
XLA Modules:
  0.0 356.0 jit_solution(9226249464720542112)
XLA Ops:
  7.2 0.0 reduce-scatter.13.cloned.1.call-start
  7.2 0.7 maximum_reduce_fusion
  7.9 0.1 fusion
  8.0 1.3 reshape.181.rm_ref
  9.2 1.3 reshape.166.qs_ref.sq_ref.sk_ref.sv_ref
  10.6 0.1 max.11
  10.6 0.1 lt.60
  10.7 0.1 lt.61
  10.8 0.1 lt.58
  10.9 0.6 copy.27.km_ref
  11.5 1.3 reshape.164.gain_ref
  12.8 1.3 reshape.168.os_ref
  14.1 1.3 reshape.167.qb_ref
  15.4 1.3 reshape.165.bias_ref
  16.7 58.7 %forward.1 = (bf16[1024,3840]{1,0:T(8,128)(2,1)}, f32[8,8,64,256]{3,2,1,0:T(8,128)}, bf16[1024,1280]{1,0:T(8,128)(2,1)}, bf16[1024,1280]{1,0:T(8,128)(2,1)}, bf1...) custom-call(s32[1]{0:T(128)} %bitcast.3.core_ref, bf16[1024,1280]{1,0:T(8,128)(2,1)} %bitcast.19, ...), custom_call_target="tpu_custom_call" | custom-call | flops 20000000000 | bytes 40000000 | tf_op jit(solution)/shard_map/forward/pallas_call | solution.py:164
  75.4 1.6 collective-permute-start
  77.1 3.3 collective-permute-done
  80.4 3.1 add.22
  83.5 0.0 reduce-scatter.13.cloned.1.call-update
  83.5 0.0 reduce-scatter.15.cloned.1.call-start
  83.6 28.5 %backward0.1 = (bf16[1024,640]{1,0:T(8,128)(2,1)}, bf16[1024,640]{1,0:T(8,128)(2,1)}, bf16[1024,640]{1,0:T(8,128)(2,1)}, bf16[640,1920]{1,0:T(8,128)(2,1)}, bf16[640,1920]{1,0:T(8,128)(2,1)}) custom-call(bf16[1024,3840]{1,0:T(8,128)(2,1)} %get-tuple-element.24.q_ref.k_ref.v_ref, bf16[1024,3840]{1,0:T(8,128)(2,1)} %get-tuple-element.24.q_ref.k_ref.v_ref, ...), custom_call_target="tpu_custom_call" | custom-call | flops 8000000000 | bytes 30000000 | tf_op jit(solution)/shard_map/backward0/pallas_call | solution.py:258
  112.0 0.3 collective-permute-start.1
  112.4 4.5 %collective-permute-done.1 = bf16[640,1920]{1,0:T(8,128)(2,1)S(1)} collective-permute-done((bf16[640,1920]{1,0:T(8,128)(2,1)}, bf16[640,1920]{1,0:T(8,128)(2,1)S(1)}, u32[]{:S(2)}, u32[]{:S(2)}) %collective-permute-start.1) | collective-permute-done | bytes 2457632 | tf_op jit(solution)/shard_map/ppermute | solution.py:346
  116.9 3.8 %add.23 = bf16[640,1920]{1,0:T(8,128)(2,1)} add(bf16[640,1920]{1,0:T(8,128)(2,1)} %get-tuple-element.38, bf16[640,1920]{1,0:T(8,128)(2,1)S(1)} %collective-permute-done.1) | non-fusion elementwise | flops 1228800 | bytes 7372800 | tf_op jit(solution)/shard_map/add | solution.py:347
  120.7 0.0 reduce-scatter.15.cloned.1.call-update
  120.7 0.0 reduce-scatter.17.cloned.1.call-start
  120.8 28.5 %backward1.1 = (bf16[1024,640]{1,0:T(8,128)(2,1)}, bf16[1024,640]{1,0:T(8,128)(2,1)}, bf16[1024,640]{1,0:T(8,128)(2,1)}, bf16[640,1920]{1,0:T(8,128)(2,1)}, bf16[640,1920]{1,0:T(8,128)(2,1)}) custom-call(bf16[1024,3840]{1,0:T(8,128)(2,1)} %get-tuple-element.24.q_ref.k_ref.v_ref, bf16[1024,3840]{1,0:T(8,128)(2,1)} %get-tuple-element.24.q_ref.k_ref.v_ref, ...), custom_call_target="tpu_custom_call" | custom-call | flops 8000000000 | bytes 30000000 | tf_op jit(solution)/shard_map/backward1/pallas_call | solution.py:258
  149.3 0.2 collective-permute-start.2
  149.6 4.7 %collective-permute-done.2 = bf16[640,1920]{1,0:T(8,128)(2,1)S(1)} collective-permute-done((bf16[640,1920]{1,0:T(8,128)(2,1)}, bf16[640,1920]{1,0:T(8,128)(2,1)S(1)}, u32[]{:S(2)}, u32[]{:S(2)}) %collective-permute-start.2) | collective-permute-done | bytes 2457632 | tf_op jit(solution)/shard_map/ppermute | solution.py:346
  154.2 3.8 %add.24 = bf16[640,1920]{1,0:T(8,128)(2,1)} add(bf16[640,1920]{1,0:T(8,128)(2,1)} %get-tuple-element.40, bf16[640,1920]{1,0:T(8,128)(2,1)S(1)} %collective-permute-done.2) | non-fusion elementwise | flops 1228800 | bytes 7372800 | tf_op jit(solution)/shard_map/add | solution.py:347
  158.0 0.0 reduce-scatter.17.cloned.1.call-update
  158.0 0.0 copy-start
  158.1 0.3 reduce-scatter.11.cloned.1.call-start
  158.3 0.6 reduce-scatter.13.cloned.1.call-done
  158.9 0.9 concatenate.17
  159.8 78.1 %reduce-scatter.15.cloned.1.call-done = bf16[1,40,1920]{2,1,0:T(8,128)(2,1)} async-done(((bf16[16,40,1920]{2,1,0:T(8,128)(2,1)}), bf16[1,40,1920]{2,1,0:T(8,128)(2,1)}) %reduce-scatter.15.cloned.1.call-update) | async-done | bytes 153616
  237.9 1.0 concatenate.18
  238.9 78.1 %reduce-scatter.17.cloned.1.call-done = bf16[1,40,1920]{2,1,0:T(8,128)(2,1)} async-done(((bf16[16,40,1920]{2,1,0:T(8,128)(2,1)}), bf16[1,40,1920]{2,1,0:T(8,128)(2,1)}) %reduce-scatter.17.cloned.1.call-update) | async-done | bytes 153616
  317.0 1.0 concatenate.19
  317.9 1.2 maximum_convert_fusion
  319.1 0.0 reduce-scatter.11.cloned.1.call-update
  319.1 0.0 copy-done
  319.1 0.6 reshape.169.ob_ref
  319.7 26.2 %finish.1 = (bf16[1024,1280]{1,0:T(8,128)(2,1)}, bf16[1024,1280]{1,0:T(8,128)(2,1)}) custom-call(bf16[1024,1280]{1,0:T(8,128)(2,1)} %bitcast.20, bf16[1024,1280]{1,0:T(8,128)(2,1)} %bitcast.22, f32[1024,1]{1,0:T(8,128)} %reshape.181.rm_ref, bf16[1024,1280]{1,0:T(8,128)(2,1)} %get-tuple-element.23.att_ref, bf16[1024,640]{1,0:T(8,128)(2,1)} %get-tuple-element.28.g0_ref, ...), custom_call_target="tpu_custom_call" | custom-call | flops 14000000000 | bytes 30000000 | tf_op jit(solution)/shard_map/finish/pallas_call | solution.py:319
  345.9 0.0 reduce-scatter.11.cloned.1.call-done
  346.0 1.0 slice.8
  346.9 1.5 slice.9
  348.5 0.1 reshape.175
  348.6 0.1 copy.29
  348.7 0.8 reshape.176
  (3 shorter events, 0.0 us)
Async XLA Ops:
  7.2 151.7 %reduce-scatter.13.cloned.1.call-start = ((), (), s32[]{:S(2)}) async-start(), calls=%async_computation.5 | async-start | bytes 1740800
  75.4 5.0 %collective-permute-start = (bf16[640,1280]{1,0:T(8,128)(2,1)}, bf16[640,1280]{1,0:T(8,128)(2,1)S(1)}, u32[]{:S(2)}, u32[]{:S(2)}) collective-permute-start(bf16[640,1280]{1,0:T(8,128)(2,1)} %get-tuple-element.37), channel_id=1, source_target_pairs={{0,16},{16,0},{32,48},{48,32},{64,80},{80,64},{96,112},{112,96},{1... | collective-permute-start | bytes 4915208 | tf_op jit(solution)/shard_map/ppermute | solution.py:346
  83.5 154.4 %reduce-scatter.15.cloned.1.call-start = ((), (), s32[]{:S(2)}) async-start(), calls=%async_computation.6 | async-start | bytes 2611200
  112.0 4.9 %collective-permute-start.1 = (bf16[640,1920]{1,0:T(8,128)(2,1)}, bf16[640,1920]{1,0:T(8,128)(2,1)S(1)}, u32[]{:S(2)}, u32[]{:S(2)}) collective-permute-start(bf16[640,1920]{1,0:T(8,128)(2,1)} %get-tuple-element.39), channel_id=1, source_target_pairs={{0,16},{16,0},{32,48},{48,32},{64,80},{80,64},{96,112},{112,96},{1... | collective-permute-start | bytes 7372808 | tf_op jit(solution)/shard_map/ppermute | solution.py:346
  120.7 196.2 %reduce-scatter.17.cloned.1.call-start = ((), (), s32[]{:S(2)}) async-start(), calls=%async_computation.7 | async-start | bytes 2611200
  149.3 4.9 %collective-permute-start.2 = (bf16[640,1920]{1,0:T(8,128)(2,1)}, bf16[640,1920]{1,0:T(8,128)(2,1)S(1)}, u32[]{:S(2)}, u32[]{:S(2)}) collective-permute-start(bf16[640,1920]{1,0:T(8,128)(2,1)} %get-tuple-element.41), channel_id=1, source_target_pairs={{0,16},{16,0},{32,48},{48,32},{64,80},{80,64},{96,112},{112,96},{1... | collective-permute-start | bytes 7372808 | tf_op jit(solution)/shard_map/ppermute | solution.py:346
  158.0 161.1 %copy-start = (f32[1280]{0:T(1024)S(1)}, f32[1280]{0:T(1024)}, u32[]{:S(2)}) copy-start(f32[1280]{0:T(1024)} %param.23) | copy-start | bytes 15364
  158.1 187.9 %reduce-scatter.11.cloned.1.call-start = ((), (), s32[]{:S(2)}) async-start(), calls=%async_computation.4 | async-start | bytes 1638400 | tf_op jit(solution)/shard_map/reduce_scatter | solution.py:379
Sparse Core Ops, SparseCore 0:
  83.7 75.1 reduce-scatter.12
  162.2 75.6 reduce-scatter.14
  241.8 75.0 reduce-scatter.16
  319.2 23.0 reduce-scatter.10
